TPU v7x, 256 devices: a whole 4x4x8 slice. The times are simulated.
256 devices in a mesh: row: 8 (over z_lo, y), col: 32 (over z_hi, x, core).
Axes of the slice: x: 4, y: 4, z: 8 (z_hi: 4, z_lo: 2; z = z_hi * 2 + z_lo), core: 2. Of those that a mesh axis runs over, the one named last changes fastest.
Arguments:
- points: float32 [16, 32768], P(None, ('row', 'col')), may hold values from -6 to 6
- inverse_length: float32 [16], replicated, may hold values from 0.35 to 1.4
- target: float32 [32768], P(('row', 'col')), may hold values from -6 to 6
- probe_bits: int32 [15, 32768], P(None, ('row', 'col')), may hold values from 0 to 1
- leaf_inverse: float32 [32768, 128], P(('row', 'col')), may hold values from -1 to 4, as said below
- top_basis: float32 [64, 32768], P(None, ('row', 'col')), may hold values from -0.09375 to 0.09375
- sub_basis: float32 [64, 32768], P(None, ('row', 'col')), may hold values from -0.1875 to 0.1875
Outputs:
- solution: float32 [16, 32768], P(None, ('row', 'col'))
- residual: float32 [16, 32768], P(None, ('row', 'col'))
- coefficients: float32 [2, 2, 16], replicated
Inputs may be any that keep to these rules, and one draw needn't show every extreme that they name: `leaf_inverse`: each leaf block is symmetric, and each of its diagonal entries exceeds the sum of the absolute values of the other entries of its row.
All inputs are finite; a program needn't handle non-finite values.
Results may differ from a plain program's by a relative error of at most 0.0003.
Values sent between devices are 32-bit elements; how exact they have to be, the bound alone decides.
No kernel may reach another device: no remote copies, remote signals or barrier semaphores. Data moves between devices by JAX's collectives and lax.ppermute only.
A program may use at most 64 MiB of HBM per device.

v0:
```python
import math

import jax
import jax.numpy as jnp
from jax import lax
from jax.sharding import PartitionSpec as P

ITERS = 2


root_five = math.sqrt(5.0)
noise_level = 0.5


def matern_block(left, right):
    left_sq = jnp.sum(left * left, 0)
    right_sq = jnp.sum(right * right, 0)
    cross = lax.dot_general(
        left,
        right,
        (((0,), (0,)), ((), ())),
        precision=lax.Precision.HIGHEST,
        preferred_element_type=jnp.float32,
    )
    dist_sq = jnp.maximum(left_sq[:, None] + right_sq[None, :] - 2.0 * cross, 0.0)
    dist = jnp.sqrt(dist_sq)
    return (1.0 + root_five * dist + 5.0 / 3.0 * dist_sq) * jnp.exp(-root_five * dist)


def split_blocks(array, width):
    return array.reshape(array.shape[0], array.shape[1] // width, width).transpose(1, 0, 2)


def on_device(points, inverse_length, target, probe_bits, leaf_inverse, top_basis, sub_basis):
    scaled = points * inverse_length[:, None]
    signs = 2.0 * probe_bits.astype(jnp.float32) - 1.0
    rhs = jnp.concatenate([target[None, :], signs], axis=0)
    cols = rhs.shape[0]
    own_rows = rhs.shape[1]
    row_pts = lax.all_gather(scaled, "col", axis=1, tiled=True)
    col_pts = lax.all_gather(scaled, "row", axis=1, tiled=True)
    group = math.gcd(own_rows, 8)

    def apply_precond(vectors):
        leaf_part = lax.dot_general(
            vectors,
            leaf_inverse,
            (((1,), (1,)), ((), ())),
            precision=lax.Precision.HIGHEST,
            preferred_element_type=jnp.float32,
        )
        top_local = lax.dot_general(
            top_basis,
            vectors,
            (((1,), (1,)), ((), ())),
            precision=lax.Precision.HIGHEST,
            preferred_element_type=jnp.float32,
        )
        sub_local = lax.dot_general(
            sub_basis,
            vectors,
            (((1,), (1,)), ((), ())),
            precision=lax.Precision.HIGHEST,
            preferred_element_type=jnp.float32,
        )
        top_coef = lax.psum(top_local, ("row", "col"))
        sub_coef = lax.psum(sub_local, "col")
        result = leaf_part + lax.dot_general(
            top_coef,
            top_basis,
            (((0,), (0,)), ((), ())),
            precision=lax.Precision.HIGHEST,
            preferred_element_type=jnp.float32,
        )
        result = result + lax.dot_general(
            sub_coef,
            sub_basis,
            (((0,), (0,)), ((), ())),
            precision=lax.Precision.HIGHEST,
            preferred_element_type=jnp.float32,
        )
        product = lax.psum(jnp.sum(vectors * result, 1), ("row", "col"))
        return (result, product)

    solution = jnp.zeros_like(rhs)
    residual = rhs
    precond, rz_now = apply_precond(residual)
    direction = precond
    alphas = []
    betas = []
    for step in range(ITERS):
        col_dirs = lax.all_gather(direction, "row", axis=1, tiled=True)
        npoint = lax.axis_size("col") * (own_rows // group) * group
        width = math.gcd(npoint, 1024)

        def one_block(block_pts):
            kmat = matern_block(block_pts, col_pts)
            return lax.dot_general(
                kmat,
                col_dirs,
                (((1,), (1,)), ((), ())),
                precision=lax.Precision.HIGHEST,
                preferred_element_type=jnp.float32,
            )

        packed = lax.psum_scatter(
            lax.map(one_block, split_blocks(row_pts, width)).reshape(
                lax.axis_size("col") * (own_rows // group), group * cols
            ),
            "col",
            scatter_dimension=0,
            tiled=True,
        )
        image = packed.reshape(own_rows, cols).T + noise_level * direction
        curv = lax.psum(jnp.sum(direction * image, 1), ("row", "col"))
        alpha = rz_now / curv
        solution = solution + alpha[:, None] * direction
        residual = residual - alpha[:, None] * image
        precond, rz_next = apply_precond(residual)
        beta = rz_next / rz_now
        direction = precond + beta[:, None] * direction
        rz_now = rz_next
        alphas.append(alpha)
        betas.append(beta)
    coefficients = jnp.stack([jnp.stack(alphas), jnp.stack(betas)])
    return (solution, residual, coefficients)


def solution(mesh):
    return jax.shard_map(
        on_device,
        mesh=mesh,
        in_specs=(
            P(None, ("row", "col")),
            P(),
            P(("row", "col")),
            P(None, ("row", "col")),
            P(("row", "col"), None),
            P(None, ("row", "col")),
            P(None, ("row", "col")),
        ),
        out_specs=(P(None, ("row", "col")), P(None, ("row", "col")), P()),
        check_vma=False,
    )
```

profile of v0, /device:TPU:1, one launch (start us, length us, event | category | flops | bytes accessed | tf_op | source)
XLA Modules:
  0.0 1142.3 jit_solution(1506372648231903470)
XLA Ops:
  8.0 23.8 %all_gather.13 = f32[16,1024]{1,0:T(8,128)S(1)} all-gather(f32[16,128]{1,0:T(8,128)S(1)} %broadcast_multiply_fusion), channel_id=1, replica_groups=mesh['row'=8,'col'=32] {'row'}, dimensions={1}, use_global_device_ids=true | all-gather | bytes 73728 | tf_op jit(solution)/shard_map/all_gather | solution.py:41
  31.8 53.8 %all_gather.12 = f32[16,4096]{1,0:T(8,128)S(1)} all-gather(f32[16,128]{1,0:T(8,128)S(1)} %broadcast_multiply_fusion), channel_id=1, replica_groups=mesh['row'=8,'col'=32] {'col'}, dimensions={1}, use_global_device_ids=true | all-gather | bytes 270336 | tf_op jit(solution)/shard_map/all_gather | solution.py:40
  87.1 73.6 %psum.77 = f32[64,16]{0,1:T(8,128)S(1)} all-reduce(f32[64,16]{0,1:T(8,128)S(1)} %convolution_bitcast_fusion.5), channel_id=1, replica_groups=mesh['row'=8,'col'=32] {'row','col'}, use_global_device_ids=true, to_apply=%region_0.0 | all-reduce | flops 1024 | bytes 8192 | tf_op jit(solution)/shard_map/psum | solution.py:66
  162.5 70.9 %psum.78 = f32[64,16]{0,1:T(8,128)S(1)} all-reduce(f32[64,16]{0,1:T(8,128)S(1)} %convolution_bitcast_fusion.4), channel_id=1, replica_groups=mesh['row'=8,'col'=32] {'col'}, use_global_device_ids=true, to_apply=%region_1.0 | all-reduce | flops 1024 | bytes 8192 | tf_op jit(solution)/shard_map/psum | solution.py:67
  235.2 22.5 %all_gather.14 = f32[16,1024]{1,0:T(8,128)S(1)} all-gather(f32[16,128]{1,0:T(8,128)S(1)} %convolution_add_fusion.4), channel_id=1, replica_groups=mesh['row'=8,'col'=32] {'row'}, dimensions={1}, use_global_device_ids=true | all-gather | bytes 73728 | tf_op jit(solution)/shard_map/all_gather | solution.py:92
  257.8 39.1 %while.24 = (s32[]{:T(128)}, f32[4,1024,16]{1,2,0:T(8,128)S(1)}, f32[4,16,1024]{2,1,0:T(8,128)S(1)}, f32[1024]{0:T(1024)S(1)}, f32[16,1024]{1,0:T(8,128)S(1)}, /*index=5*/f32[16,1024]{1,0:T(8,128)S(1)}, s32[]{:T(128)}) while((s32[]{:T(128)}, f32[4,1024,16]{1,2,0:T(8,128)S(1)}, f32[4,16,1024]{2,1,0:T(8,128)S(1)}, f32[1024]{0:T(1024)S(1)}, ...), condition=%wide.region_7.8_spmd, body=%wide.region_5.7_spmd.sunk | while | flops 413170688 | bytes 8728665 | solution.py:107
  261.4 6.2 fusion.135
  267.6 3.5 fusion.133
  271.1 6.2 fusion.135
  277.4 3.5 fusion.133
  280.9 6.2 fusion.135
  287.1 3.5 fusion.133
  290.7 6.2 fusion.135
  298.9 90.1 %reduce-scatter.3.cloned.1.call-done = f32[16,128]{1,0:T(8,128)} async-done(((f32[512,128]{1,0:T(8,128)}), f32[16,128]{1,0:T(8,128)}) %reduce-scatter.3.cloned.1.call-update) | async-done | bytes 8208 | tf_op jit(solution)/shard_map/reduce_scatter | solution.py:106
  389.9 75.8 %all-reduce = (f32[16]{0:T(128)S(1)}, f32[16]{0:T(128)S(1)}) all-reduce(f32[16]{0:T(128)S(1)} %get-tuple-element.138, f32[16]{0:T(128)S(1)} %get-tuple-element.137), channel_id=1, replica_groups=mesh['row'=8,'col'=32] {'row','col'}, use_global_device_ids=true, to_apply=%region_3.0 | all-reduce | flops 32 | bytes 256 | tf_op jit(solution)/shard_map/psum | solution.py:82
  466.4 73.6 %psum.81 = f32[64,16]{0,1:T(8,128)S(1)} all-reduce(f32[64,16]{0,1:T(8,128)S(1)} %convolution_bitcast_fusion.3), channel_id=1, replica_groups=mesh['row'=8,'col'=32] {'row','col'}, use_global_device_ids=true, to_apply=%region_11.12 | all-reduce | flops 1024 | bytes 8192 | tf_op jit(solution)/shard_map/psum | solution.py:66
  540.0 70.9 %psum.82 = f32[64,16]{0,1:T(8,128)S(1)} all-reduce(f32[64,16]{0,1:T(8,128)S(1)} %convolution_bitcast_fusion.2), channel_id=1, replica_groups=mesh['row'=8,'col'=32] {'col'}, use_global_device_ids=true, to_apply=%region_12.13 | all-reduce | flops 1024 | bytes 8192 | tf_op jit(solution)/shard_map/psum | solution.py:67
  611.3 74.0 %psum.83 = f32[16]{0:T(128)S(1)} all-reduce(f32[16]{0:T(128)S(1)} %get-tuple-element.167), channel_id=1, replica_groups=mesh['row'=8,'col'=32] {'row','col'}, use_global_device_ids=true, to_apply=%region_14.15 | all-reduce | flops 16 | bytes 128 | tf_op jit(solution)/shard_map/psum | solution.py:82
  685.3 22.0 %all_gather.15 = f32[16,1024]{1,0:T(8,128)S(1)} all-gather(f32[16,128]{1,0:T(8,128)S(1)} %multiply_add_fusion.1), channel_id=1, replica_groups=mesh['row'=8,'col'=32] {'row'}, dimensions={1}, use_global_device_ids=true | all-gather | bytes 73728 | tf_op jit(solution)/shard_map/all_gather | solution.py:92
  707.4 39.1 %while.25 = (s32[]{:T(128)}, f32[4,1024,16]{1,2,0:T(8,128)S(1)}, f32[4,16,1024]{2,1,0:T(8,128)S(1)}, f32[1024]{0:T(1024)S(1)}, f32[16,1024]{1,0:T(8,128)S(1)}, /*index=5*/f32[16,1024]{1,0:T(8,128)S(1)}, s32[]{:T(128)}) while((s32[]{:T(128)}, f32[4,1024,16]{1,2,0:T(8,128)S(1)}, f32[4,16,1024]{2,1,0:T(8,128)S(1)}, f32[1024]{0:T(1024)S(1)}, ...), condition=%wide.region_17.18_spmd, body=%wide.region_15.17_spmd.sunk | while | flops 413170688 | bytes 8728665 | solution.py:107
  711.0 6.2 fusion.142
  717.2 3.5 fusion.140
  720.7 6.2 fusion.142
  727.0 3.5 fusion.140
  730.5 6.2 fusion.142
  736.7 3.5 fusion.140
  740.3 6.2 fusion.142
  748.4 89.8 %reduce-scatter.5.cloned.1.call-done = f32[16,128]{1,0:T(8,128)} async-done(((f32[512,128]{1,0:T(8,128)}), f32[16,128]{1,0:T(8,128)}) %reduce-scatter.5.cloned.1.call-update) | async-done | bytes 8208 | tf_op jit(solution)/shard_map/reduce_scatter | solution.py:106
  839.1 75.8 %psum.84 = f32[16]{0:T(128)S(1)} all-reduce(f32[16]{0:T(128)S(1)} %multiply_reduce_fusion.1), channel_id=1, replica_groups=mesh['row'=8,'col'=32] {'row','col'}, use_global_device_ids=true, to_apply=%region_20.21 | all-reduce | flops 16 | bytes 128 | tf_op jit(solution)/shard_map/psum | solution.py:115
  916.2 73.5 %psum.85 = f32[64,16]{0,1:T(8,128)S(1)} all-reduce(f32[64,16]{0,1:T(8,128)S(1)} %convolution_bitcast_fusion.1), channel_id=1, replica_groups=mesh['row'=8,'col'=32] {'row','col'}, use_global_device_ids=true, to_apply=%region_21.22 | all-reduce | flops 1024 | bytes 8192 | tf_op jit(solution)/shard_map/psum | solution.py:66
  989.7 70.9 %psum.86 = f32[64,16]{0,1:T(8,128)S(1)} all-reduce(f32[64,16]{0,1:T(8,128)S(1)} %convolution_bitcast_fusion), channel_id=1, replica_groups=mesh['row'=8,'col'=32] {'col'}, use_global_device_ids=true, to_apply=%region_22.23 | all-reduce | flops 1024 | bytes 8192 | tf_op jit(solution)/shard_map/psum | solution.py:67
  1061.0 73.9 %psum.87 = f32[16]{0:T(128)S(1)} all-reduce(f32[16]{0:T(128)S(1)} %fusion.77), channel_id=1, replica_groups=mesh['row'=8,'col'=32] {'row','col'}, use_global_device_ids=true, to_apply=%region_24.25 | all-reduce | flops 16 | bytes 128 | tf_op jit(solution)/shard_map/psum | solution.py:82
  (65 shorter events, 22.3 us)
Async XLA Ops:
  7.2 153.6 %copy-start = (f32[128,128]{1,0:T(8,128)S(1)}, f32[128,128]{1,0:T(8,128)}, u32[]{:S(2)}) copy-start(f32[128,128]{1,0:T(8,128)} %param.15) | copy-start | bytes 196612
  7.2 381.8 %reduce-scatter.3.cloned.1.call-start = ((), (), s32[]{:S(2)}) async-start(), calls=%async_computation.2 | async-start | bytes 270336 | tf_op jit(solution)/shard_map/reduce_scatter | solution.py:106
  296.9 92.9 %copy-start.4 = (f32[128]{0:T(128)S(1)}, f32[128]{0:T(128)}, u32[]{:S(2)}) copy-start(f32[128]{0:T(128)} %param.13) | copy-start | bytes 1540
  296.9 168.9 %copy-start.1 = (f32[64,128]{1,0:T(8,128)S(1)}, f32[64,128]{1,0:T(8,128)}, u32[]{:S(2)}) copy-start(f32[64,128]{1,0:T(8,128)} %param.16) | copy-start | bytes 98308
  297.0 169.2 %copy-start.2 = (f32[64,128]{1,0:T(8,128)S(1)}, f32[64,128]{1,0:T(8,128)}, u32[]{:S(2)}) copy-start(f32[64,128]{1,0:T(8,128)} %param.17) | copy-start | bytes 98308
  298.8 539.3 %reduce-scatter.5.cloned.1.call-start = ((), (), s32[]{:S(2)}) async-start(), calls=%async_computation.3 | async-start | bytes 270336 | tf_op jit(solution)/shard_map/reduce_scatter | solution.py:106
  915.6 219.8 %copy-start.3 = (f32[16,128]{1,0:T(8,128)}, f32[16,128]{1,0:T(8,128)S(1)}, u32[]{:S(2)}) copy-start(f32[16,128]{1,0:T(8,128)S(1)} %get-tuple-element.165) | copy-start | bytes 24580
Sparse Core Ops, SparseCore 0:
  299.0 89.9 reduce-scatter.2
  748.5 89.5 reduce-scatter.4
where the time goes:
time: 1140 us
  blocking collectives  855 us (75%)
  waiting for transfers between devices  180 us (16%)
  matrix products  84.2 us (7%)
  between operations  14.2 us (1%)
    psum x3, blocking collectives, apply_precond(): product = lax.psum(jnp.sum(vectors * result, 1), ('row', 'col'))  224 us
    psum x3, blocking collectives, apply_precond(): top_coef = lax.psum(top_local, ('row', 'col'))  221 us
    psum x3, blocking collectives, apply_precond(): sub_coef = lax.psum(sub_local, 'col')  213 us
    reduce_scatter x2, waiting for transfers between devices, on_device(): lax.psum_scatter(lax.map(one_block, split_blocks(row_pts, width)).reshape...  180 us
    psum x1, blocking collectives, on_device(): curv = lax.psum(jnp.sum(direction * image, 1), ('row', 'col'))  75.8 us
    all_gather x1, blocking collectives, on_device(): row_pts = lax.all_gather(scaled, 'col', axis=1, tiled=True)  53.8 us
    dot_general x8, matrix products, one_block(): lax.dot_general(kmat, col_dirs, (((1,), (1,)), ((), ())), precision=lax.P...  49.7 us
    all_gather x2, blocking collectives, on_device(): col_dirs = lax.all_gather(direction, 'row', axis=1, tiled=True)  44.5 us
  transfers between devices with their start and end apart: 2, of which 2 were waited for; matrix products, arithmetic and copies ran while one was open for 0% of the time, Pallas kernels for 0%

commit v1 on v0

v1 whole, which is shorter than its diff:
```python
import functools
import math

import jax
import jax.numpy as jnp
from jax import lax
from jax.experimental import pallas as pl
from jax.experimental.pallas import tpu as pltpu
from jax.sharding import Mesh
from jax.sharding import PartitionSpec as P

AXES = ("zl", "y", "zh", "x", "c")
G1 = ("zh", "x")
G2 = ("zl", "y", "c")
NG = 16
NT = 8
COLS = 16
PTS = 128
RANK = 64
NOISE = 0.5
F32 = jnp.float32
BF16 = jnp.bfloat16
LN2 = math.log(2.0)
COORD_SCALE = math.sqrt(5.0) / LN2
HIGHEST = lax.Precision.HIGHEST


def dot_nt(a, b):
    return lax.dot_general(a, b, (((1,), (1,)), ((), ())), precision=HIGHEST, preferred_element_type=F32)


def dot_nn(a, b):
    return lax.dot_general(a, b, (((1,), (0,)), ((), ())), precision=HIGHEST, preferred_element_type=F32)


def lane(shape):
    return lax.broadcasted_iota(jnp.int32, shape, 1)


def sublane(shape):
    return lax.broadcasted_iota(jnp.int32, shape, 0)


def pack(sums):
    shape = (COLS, PTS)
    acc = jnp.zeros(shape, F32)
    for k, s in enumerate(sums):
        acc = jnp.where(lane(shape) == COLS * k + sublane(shape), jnp.broadcast_to(s, shape), acc)
    return jnp.sum(acc, 0, keepdims=True)


def unpack(row, k):
    shape = (COLS, PTS)
    hit = lane(shape) == COLS * k + sublane(shape)
    return jnp.sum(jnp.where(hit, jnp.broadcast_to(row, shape), 0.0), 1, keepdims=True)


def rowdot(a, b):
    return jnp.sum(a * b, 1, keepdims=True)


def tile_rows(rows):
    shape = (8, PTS)
    out = jnp.zeros(shape, F32)
    for k, r in enumerate(rows):
        out = jnp.where(sublane(shape) == k, jnp.broadcast_to(r, shape), out)
    return out


def tree_sum(terms):
    terms = list(terms)
    while len(terms) > 1:
        terms = [terms[i] + terms[i + 1] if i + 1 < len(terms) else terms[i] for i in range(0, len(terms), 2)]
    return terms[0]


def call(kernel, outs, *args, smem=0, limit=8 << 20, scratch=(), name=None):
    specs = [pl.BlockSpec(memory_space=pltpu.SMEM)] * smem
    specs += [pl.BlockSpec(memory_space=pltpu.VMEM)] * (len(args) - smem)
    return pl.pallas_call(
        kernel,
        out_shape=[jax.ShapeDtypeStruct(s, d) for s, d in outs],
        in_specs=specs,
        out_specs=[pl.BlockSpec(memory_space=pltpu.VMEM)] * len(outs),
        scratch_shapes=list(scratch),
        compiler_params=pltpu.CompilerParams(vmem_limit_bytes=limit),
        name=name,
    )(*args)


def start_kernel(points, inv, target, bits, top, sub, send, rhs, basis):
    rhs[0:1, :] = target[...]
    rhs[1:COLS, :] = 2.0 * bits[...].astype(F32) - 1.0
    basis[0:RANK, :] = top[...]
    basis[RANK : 2 * RANK, :] = sub[...]
    send[0:COLS, :] = points[...] * inv[...]
    send[COLS : 2 * COLS, :] = dot_nt(rhs[...], basis[...])


def fold_kernel(keep, got, own, send):
    send[...] = tree_sum([got[j] for j in range(NG)])
    if keep:
        send[0:keep, :] = own[0:keep, :]


def subtree_table(got, first, table):
    for t in range(NT):
        table[t] = got[2 * t, first : first + COLS] + got[2 * t + 1, first : first + COLS]


def own_coefs(table, mine):
    top = lane((COLS, PTS)) < RANK
    return tree_sum([jnp.where(top | (mine == t), table[t], 0.0) for t in range(NT)])


def precond0_kernel(tid, got, rhs, leaf, basis, z, table):
    subtree_table(got, COLS, table)
    coefs = own_coefs(table, tid[0])
    z[...] = dot_nt(rhs[...], leaf[...]) + dot_nn(coefs, basis[...])


def features(x, left):
    def pieces(v):
        first = v.astype(BF16).astype(F32)
        second = (v - first).astype(BF16).astype(F32)
        third = (v - first - second).astype(BF16).astype(F32)
        return first, second, third

    a, b, c = pieces(x)
    norms = pieces(jnp.sum(x * x, 0, keepdims=True))
    ones = (jnp.ones((1, PTS), F32),) * 3
    if left:
        parts = [a, a, b, b, a, c]
        tail = tile_rows(norms + ones)
    else:
        a, b, c = -2.0 * a, -2.0 * b, -2.0 * c
        parts = [a, b, a, b, c, a]
        tail = tile_rows(ones + norms)
    return jnp.concatenate(parts + [tail, jnp.zeros((PTS - 6 * COLS - 8, PTS), F32)], 0)


def matern_kernel(left, right, high, low, left_f, right_f):
    for j in range(NG):
        at = slice(j * PTS, (j + 1) * PTS)
        right_f[:, at] = features(right[j, 0:COLS] * COORD_SCALE, False).astype(BF16)
        left_f[at, :] = features(left[j, 0:COLS] * COORD_SCALE, True).T.astype(BF16)
    width = 256

    def step(i, carry):
        rows = pl.ds(pl.multiple_of(i * PTS, PTS), PTS)
        lhs = left_f[rows, :]
        for j in range(0, NG * PTS, width):
            s = jnp.dot(lhs, right_f[:, j : j + width], preferred_element_type=F32)
            s = jnp.maximum(s, 1e-30)
            v = s * lax.rsqrt(s)
            k = ((LN2 * LN2 / 3.0 * s + 1.0) + LN2 * v) * jnp.exp2(-v)
            h = k.astype(BF16)
            high[rows, j : j + width] = h
            low[rows, j : j + width] = (k - h.astype(F32)).astype(BF16)
        return carry

    lax.fori_loop(0, NG, step, 0)


def matvec_kernel(got, high, low, out):
    v = jnp.concatenate([got[j] for j in range(NG)], 1)
    v_high = v.astype(BF16)
    both = jnp.concatenate([v_high, (v - v_high.astype(F32)).astype(BF16)], 0)
    width = 512
    for j in range(0, NG * PTS, width):
        r = jnp.dot(both, high[:, j : j + width], preferred_element_type=F32)
        r = r[0:COLS] + r[COLS:] + jnp.dot(v_high, low[:, j : j + width], preferred_element_type=F32)
        for b in range(width // PTS):
            out[j // PTS + b] = r[:, b * PTS : (b + 1) * PTS]


def image0_kernel(got, z, rhs, basis, q, send):
    q[...] = tree_sum([got[j] for j in range(NG)]) + NOISE * z[...]
    send[0:COLS, :] = dot_nt(q[...], basis[...])
    send[COLS:, :] = tile_rows([pack([rowdot(rhs[...], z[...]), rowdot(z[...], q[...])])])


def precond1_kernel(tid, got, rhs, q, leaf, basis, table0, z, res, table, table_q, sums):
    sums[...] = tree_sum([got[j, COLS:] for j in range(NG)])
    alpha = unpack(sums[0:1, :], 0) / unpack(sums[0:1, :], 1)
    subtree_table(got, 0, table_q)
    for t in range(NT):
        table[t] = table0[t] - alpha * table_q[t]
    coefs = own_coefs(table, tid[0])
    res[...] = rhs[...] - alpha * q[...]
    z[...] = dot_nt(res[...], leaf[...]) + dot_nn(coefs, basis[...])


def image1_kernel(got, z1, z0, res, q, leaf, basis, p, send):
    p[...] = tree_sum([got[j] for j in range(NG)]) + NOISE * z1[...]
    send[0:COLS, :] = dot_nt(p[...], basis[...])
    rv, qv, pv, zv = res[...], q[...], p[...], z1[...]
    rb, qb, pb = (dot_nt(v, leaf[...]) for v in (rv, qv, pv))
    first = pack([rowdot(rv, zv), rowdot(zv, pv), rowdot(zv, qv), rowdot(z0[...], pv)])
    second = pack([rowdot(rv, rb), rowdot(rv, qb), rowdot(rv, pb), rowdot(qv, qb), rowdot(qv, pb), rowdot(pv, pb)])
    send[COLS:, :] = tile_rows([first, second])


def finish_kernel(got, z0, z1, res, q, p, table1, table_q, sums0, x_out, r_out, coefs):
    sums = tree_sum([got[j, COLS:] for j in range(NG)])
    rz0, z0q = unpack(sums0[0:1, :], 0), unpack(sums0[0:1, :], 1)
    rz1, z1p, z1q, z0p = (unpack(sums[0:1, :], k) for k in range(4))
    rbr, rbq, rbp, qbq, qbp, pbp = (unpack(sums[1:2, :], k) for k in range(6))
    alpha0 = rz0 / z0q
    beta0 = rz1 / rz0
    alpha1 = rz1 / (z1p + beta0 * (z1q + z0p) + beta0 * beta0 * z0q)
    image = p[...] + beta0 * q[...]
    r_out[...] = res[...] - alpha1 * image
    x_out[...] = alpha0 * z0[...] + alpha1 * (z1[...] + beta0 * z0[...])
    leaf_part = (
        rbr
        - 2.0 * alpha1 * (rbp + beta0 * rbq)
        + alpha1 * alpha1 * (pbp + 2.0 * beta0 * qbp + beta0 * beta0 * qbq)
    )
    top = lane((COLS, PTS)) < RANK
    now = [
        table1[t] - alpha1 * (got[2 * t, 0:COLS] + got[2 * t + 1, 0:COLS] + beta0 * table_q[t]) for t in range(NT)
    ]
    whole = jnp.where(top, tree_sum(now), 0.0)
    squares = whole * whole + tree_sum([jnp.where(top, 0.0, v * v) for v in now])
    beta1 = (leaf_part + jnp.sum(squares, 1, keepdims=True)) / rz1
    for k, v in enumerate((alpha0, alpha1, beta0, beta1)):
        coefs[k // 2, k % 2 : k % 2 + 1, :] = pack([v])[:, 0:COLS]


def gather(block, axes):
    return lax.all_to_all(jnp.broadcast_to(block[None], (NG,) + block.shape), axes, 0, 0, tiled=True)


def on_device(points, inverse_length, target, probe_bits, leaf, top_basis, sub_basis):
    vec = ((COLS, PTS), F32)
    table = ((NT, COLS, PTS), F32)
    block = ((NG * PTS, NG * PTS), BF16)
    tid = lax.axis_index(("zl", "y")).astype(jnp.int32).reshape(1)
    send, rhs, basis = call(
        start_kernel,
        [((2 * COLS, PTS), F32), vec, ((2 * RANK, PTS), F32)],
        points, inverse_length[:, None], target[None, :], probe_bits, top_basis, sub_basis,
        name="start",
    )
    got1 = gather(send, G1)
    (send,) = call(functools.partial(fold_kernel, COLS), [((2 * COLS, PTS), F32)], got1, send, name="fold0")
    got2 = gather(send, G2)
    z0, table0 = call(precond0_kernel, [vec, table], tid, got2, rhs, leaf, basis, smem=1, name="precond0")
    dirs = gather(z0, G1)
    high, low = call(
        matern_kernel, [block, block], got1, got2,
        limit=24 << 20,
        scratch=[pltpu.VMEM((NG * PTS, PTS), BF16), pltpu.VMEM((PTS, NG * PTS), BF16)],
        name="matern",
    )

    def matvec(dirs):
        (parts,) = call(matvec_kernel, [((NG, COLS, PTS), F32)], dirs, high, low, limit=24 << 20, name="matvec")
        return lax.all_to_all(parts, G2, 0, 0, tiled=True)

    wide = ((COLS + 8, PTS), F32)
    q, send = call(image0_kernel, [vec, wide], matvec(dirs), z0, rhs, basis, name="image0")
    (send,) = call(functools.partial(fold_kernel, 0), [wide], gather(send, G1), send, name="fold1")
    z1, res, table1, table_q, sums0 = call(
        precond1_kernel, [vec, vec, table, table, ((8, PTS), F32)],
        tid, gather(send, G2), rhs, q, leaf, basis, table0, smem=1, name="precond1",
    )
    p, send = call(
        image1_kernel, [vec, wide], matvec(gather(z1, G1)), z1, z0, res, q, leaf, basis, name="image1"
    )
    (send,) = call(functools.partial(fold_kernel, 0), [wide], gather(send, G1), send, name="fold2")
    x_out, r_out, coefs = call(
        finish_kernel, [vec, vec, ((2, 2, COLS), F32)],
        gather(send, G2), z0, z1, res, q, p, table1, table_q, sums0, name="finish",
    )
    return x_out, r_out, coefs


def solution(mesh):
    named = Mesh(mesh.devices.reshape(2, 4, 4, 4, 2), AXES)
    return jax.shard_map(
        on_device,
        mesh=named,
        in_specs=(P(None, AXES), P(), P(AXES), P(None, AXES), P(AXES, None), P(None, AXES), P(None, AXES)),
        out_specs=(P(None, AXES), P(None, AXES), P()),
        check_vma=False,
    )
```

time: 1140 us -> 168 us (0.15)
  blocking collectives: 855 us -> 110 us
  waiting for transfers between devices: 180 us -> 7.2 us
  matrix products: 84.2 us -> 0 us
  Pallas kernels: 0 us -> 17.6 us
  local copies, waits for them, and re-layouts: 5.43 us -> 19.9 us
  between operations: 14.2 us -> 0.73 us
  starting transfers between devices: 0.08 us -> 11.8 us
    psum x10 -> x0, blocking collectives: 733 us -> none  [the longest x3 224 us: apply_precond(): product = lax.psum(jnp.sum(vectors * result, 1), ('row', 'col'))]
    reduce_scatter x2 -> x0, waiting for transfers between devices: 180 us -> none  [on_device(): lax.psum_scatter(lax.map(one_block, split_blocks(row_pts, width)).reshape...]
    all_gather x4 -> x0, blocking collectives: 122 us -> none  [the longest x1 53.8 us: on_device(): row_pts = lax.all_gather(scaled, 'col', axis=1, tiled=True)]
    all_to_all x0 -> x8, blocking collectives: none -> 110 us  [the longest x6 89.3 us: gather(): lax.all_to_all(jnp.broadcast_to(block[None], (NG,) + block.shape), axes,...]
    dot_general x31 -> x0, matrix products: 84.2 us -> none  [the longest x8 49.7 us: one_block(): lax.dot_general(kmat, col_dirs, (((1,), (1,)), ((), ())), precision=lax.P...]
    unnamed x10 -> x22, local copies, waits for them, and re-layouts: 0.03 us -> 17.6 us
    pallas_call x0 -> x12, Pallas kernels: none -> 17.6 us  [call(): pl.pallas_call(kernel, out_shape=[jax.ShapeDtypeStruct(s, d) for s, d in...]
    all_to_all x0 -> x2, starting transfers between devices: none -> 11.8 us  [gather(): lax.all_to_all(jnp.broadcast_to(block[None], (NG,) + block.shape), axes,...]
  transfers between devices with their start and end apart: 2 -> 2, of which waited for: 2 -> 1; matrix products, arithmetic and copies ran while one was open for 0% -> 0% of each run, Pallas kernels for 0% -> 6%
where the time goes in v1:
time: 168 us; the launch traced here: 167 us
  blocking collectives  110 us (65%)
  local copies, waits for them, and re-layouts  19.9 us (12%)
  Pallas kernels  17.6 us (10%)
  starting transfers between devices  11.8 us (7%)
  waiting for transfers between devices  7.2 us (4%)
    all_to_all x6, blocking collectives, gather(): lax.all_to_all(jnp.broadcast_to(block[None], (NG,) + block.shape), axes,...  89.3 us
    all_to_all x2, blocking collectives, matvec(): return lax.all_to_all(parts, G2, 0, 0, tiled=True)  20.8 us
    unnamed x22, local copies, waits for them, and re-layouts  17.6 us
    pallas_call x12, Pallas kernels, call(): pl.pallas_call(kernel, out_shape=[jax.ShapeDtypeStruct(s, d) for s, d in...  17.6 us
    all_to_all x2, starting transfers between devices, gather(): lax.all_to_all(jnp.broadcast_to(block[None], (NG,) + block.shape), axes,...  11.8 us
    all_to_all x2, waiting for transfers between devices, gather(): lax.all_to_all(jnp.broadcast_to(block[None], (NG,) + block.shape), axes,...  7.2 us
  transfers between devices with their start and end apart: 2, of which 1 were waited for; matrix products, arithmetic and copies ran while one was open for 0% of the time, Pallas kernels for 6%

profile of v1, /device:TPU:1, one launch (start us, length us, event | category | flops | bytes accessed | tf_op | source)
XLA Modules:
  0.0 167.2 jit_solution(5915013558714829064)
XLA Ops:
  0.6 0.7 copy.10.inv
  1.4 0.8 copy-done.6
  2.1 0.8 copy-done.7
  2.9 0.7 copy-done.8
  3.6 0.7 copy-done.9
  4.3 0.7 copy-done.10
  5.2 21.5 %all_to_all.50.got.left = f32[16,32,128]{2,1,0:T(8,128)S(1)} all-to-all(f32[16,32,128]{2,1,0:T(8,128)S(1)} %broadcast_in_dim.22), channel_id=1, replica_groups=mesh['zl'=2,'y'=4,'zh'=4,'x'=4,'c'=2] {'zh','x'}, dimensions={0} | all-to-all | bytes 524288 | tf_op jit(solution)/shard_map/all_to_all | solution.py:232
  26.7 0.7 broadcast_in_dim.23
  27.4 8.1 %all-to-all-start.1 = ((f32[16,32,128]{2,1,0:T(8,128)}), f32[16,32,128]{2,1,0:T(8,128)S(1)}, u32[]{:S(2)}, u32[]{:S(2)}) async-start(f32[16,32,128]{2,1,0:T(8,128)} %broadcast_in_dim.23), calls=%async_computation.1 | async-start | bytes 524288 | tf_op jit(solution)/shard_map/all_to_all | solution.py:232
  35.5 7.2 %all-to-all-done.1.got.right = f32[16,32,128]{2,1,0:T(8,128)S(1)} async-done(((f32[16,32,128]{2,1,0:T(8,128)}), f32[16,32,128]{2,1,0:T(8,128)S(1)}, u32[]{:S(2)}, u32[]{:S(2)}) %all-to-all-start.1) | async-done | bytes 262176 | tf_op jit(solution)/shard_map/all_to_all | solution.py:232
  42.7 0.8 copy-done.4
  43.5 0.3 precond0.1
  43.8 0.7 broadcast_in_dim.24
  44.5 3.7 %all-to-all-start.2 = ((f32[16,16,128]{2,1,0:T(8,128)}), f32[16,16,128]{2,1,0:T(8,128)S(1)}, u32[]{:S(2)}, u32[]{:S(2)}) async-start(f32[16,16,128]{2,1,0:T(8,128)} %broadcast_in_dim.24), calls=%async_computation.2 | async-start | bytes 262144 | tf_op jit(solution)/shard_map/all_to_all | solution.py:232
  48.2 10.2 %matern.1 = (bf16[2048,2048]{1,0:T(8,128)(2,1)S(1)}, bf16[2048,2048]{1,0:T(8,128)(2,1)S(1)}) custom-call(f32[16,32,128]{2,1,0:T(8,128)S(1)} %all_to_all.50.got.left, f32[16,32,128]{2,1,0:T(8,128)S(1)} %all-to-all-done.1.got.right), custom_call_target="tpu_custom_call" | custom-call | tf_op jit(solution)/shard_map/matern/pallas_call | solution.py:80
  58.4 3.2 %copy-done = bf16[2048,2048]{1,0:T(8,128)(2,1)} copy-done((bf16[2048,2048]{1,0:T(8,128)(2,1)}, bf16[2048,2048]{1,0:T(8,128)(2,1)S(1)}, u32[]{:S(2)}) %copy-start) | copy-done | bytes 8388632
  61.6 3.2 %copy-done.2 = bf16[2048,2048]{1,0:T(8,128)(2,1)} copy-done((bf16[2048,2048]{1,0:T(8,128)(2,1)}, bf16[2048,2048]{1,0:T(8,128)(2,1)S(1)}, u32[]{:S(2)}) %copy-start.2) | copy-done | bytes 8388632
  64.8 3.4 %copy-done.1 = bf16[2048,2048]{1,0:T(8,128)(2,1)S(1)} copy-done((bf16[2048,2048]{1,0:T(8,128)(2,1)S(1)}, bf16[2048,2048]{1,0:T(8,128)(2,1)}, u32[]{:S(2)}) %copy-start.1) | copy-done | bytes 8388632
  68.2 3.4 %copy-done.3 = bf16[2048,2048]{1,0:T(8,128)(2,1)S(1)} copy-done((bf16[2048,2048]{1,0:T(8,128)(2,1)S(1)}, bf16[2048,2048]{1,0:T(8,128)(2,1)}, u32[]{:S(2)}) %copy-start.3) | copy-done | bytes 8388632
  71.6 2.5 %matvec.2 = f32[16,16,128]{2,1,0:T(8,128)S(1)} custom-call(f32[16,16,128]{2,1,0:T(8,128)S(1)} %all-to-all-done.2.got, bf16[2048,2048]{1,0:T(8,128)(2,1)S(1)} %copy-done.1, bf16[2048,2048]{1,0:T(8,128)(2,1)S(1)} %copy-done.3), custom_call_target="tpu_custom_call" | custom-call | tf_op jit(solution)/shard_map/matvec/pallas_call | solution.py:80
  74.1 9.8 %all_to_all.51.got = f32[16,16,128]{2,1,0:T(8,128)S(1)} all-to-all(f32[16,16,128]{2,1,0:T(8,128)S(1)} %matvec.2), channel_id=1, replica_groups=mesh['zl'=2,'y'=4,'zh'=4,'x'=4,'c'=2] {'zl','y','c'}, dimensions={0} | all-to-all | bytes 262144 | tf_op jit(solution)/shard_map/all_to_all | solution.py:260
  83.9 0.2 image0.1
  84.1 18.8 %all_to_all.52.got = f32[16,24,128]{2,1,0:T(8,128)S(1)} all-to-all(f32[16,24,128]{2,1,0:T(8,128)S(1)} %broadcast_in_dim.25), channel_id=1, replica_groups=mesh['zl'=2,'y'=4,'zh'=4,'x'=4,'c'=2] {'zh','x'}, dimensions={0} | all-to-all | bytes 393216 | tf_op jit(solution)/shard_map/all_to_all | solution.py:232
  103.0 11.9 %all_to_all.53.got = f32[16,24,128]{2,1,0:T(8,128)S(1)} all-to-all(f32[16,24,128]{2,1,0:T(8,128)S(1)} %broadcast_in_dim.26), channel_id=1, replica_groups=mesh['zl'=2,'y'=4,'zh'=4,'x'=4,'c'=2] {'zl','y','c'}, dimensions={0} | all-to-all | bytes 393216 | tf_op jit(solution)/shard_map/all_to_all | solution.py:232
  114.8 0.3 precond1.1
  115.2 12.7 %all_to_all.54.got = f32[16,16,128]{2,1,0:T(8,128)S(1)} all-to-all(f32[16,16,128]{2,1,0:T(8,128)S(1)} %broadcast_in_dim.27), channel_id=1, replica_groups=mesh['zl'=2,'y'=4,'zh'=4,'x'=4,'c'=2] {'zh','x'}, dimensions={0} | all-to-all | bytes 262144 | tf_op jit(solution)/shard_map/all_to_all | solution.py:232
  127.9 2.5 %matvec.3 = f32[16,16,128]{2,1,0:T(8,128)S(1)} custom-call(f32[16,16,128]{2,1,0:T(8,128)S(1)} %all_to_all.54.got, bf16[2048,2048]{1,0:T(8,128)(2,1)S(1)} %copy-done.1, bf16[2048,2048]{1,0:T(8,128)(2,1)S(1)} %copy-done.3), custom_call_target="tpu_custom_call" | custom-call | tf_op jit(solution)/shard_map/matvec/pallas_call | solution.py:80
  130.4 10.9 %all_to_all.55.got = f32[16,16,128]{2,1,0:T(8,128)S(1)} all-to-all(f32[16,16,128]{2,1,0:T(8,128)S(1)} %matvec.3), channel_id=1, replica_groups=mesh['zl'=2,'y'=4,'zh'=4,'x'=4,'c'=2] {'zl','y','c'}, dimensions={0} | all-to-all | bytes 262144 | tf_op jit(solution)/shard_map/all_to_all | solution.py:260
  141.3 0.6 image1.1
  141.9 12.6 %all_to_all.56.got = f32[16,24,128]{2,1,0:T(8,128)S(1)} all-to-all(f32[16,24,128]{2,1,0:T(8,128)S(1)} %broadcast_in_dim.28), channel_id=1, replica_groups=mesh['zl'=2,'y'=4,'zh'=4,'x'=4,'c'=2] {'zh','x'}, dimensions={0} | all-to-all | bytes 393216 | tf_op jit(solution)/shard_map/all_to_all | solution.py:232
  154.6 11.9 %all_to_all.57.got = f32[16,24,128]{2,1,0:T(8,128)S(1)} all-to-all(f32[16,24,128]{2,1,0:T(8,128)S(1)} %broadcast_in_dim.29), channel_id=1, replica_groups=mesh['zl'=2,'y'=4,'zh'=4,'x'=4,'c'=2] {'zl','y','c'}, dimensions={0} | all-to-all | bytes 393216 | tf_op jit(solution)/shard_map/all_to_all | solution.py:232
  166.5 0.8 finish.1
  (23 shorter events, 0.4 us)
Async XLA Ops:
  1.4 0.8 copy-start.6
  2.1 0.8 copy-start.7
  2.9 0.7 copy-start.8
  3.6 0.7 copy-start.9
  4.3 0.7 copy-start.10
  27.4 15.2 %all-to-all-start.1 = ((f32[16,32,128]{2,1,0:T(8,128)}), f32[16,32,128]{2,1,0:T(8,128)S(1)}, u32[]{:S(2)}, u32[]{:S(2)}) async-start(f32[16,32,128]{2,1,0:T(8,128)} %broadcast_in_dim.23), calls=%async_computation.1 | async-start | bytes 524288 | tf_op jit(solution)/shard_map/all_to_all | solution.py:232
  42.7 0.8 copy-start.4
  44.5 20.3 %all-to-all-start.2 = ((f32[16,16,128]{2,1,0:T(8,128)}), f32[16,16,128]{2,1,0:T(8,128)S(1)}, u32[]{:S(2)}, u32[]{:S(2)}) async-start(f32[16,16,128]{2,1,0:T(8,128)} %broadcast_in_dim.24), calls=%async_computation.2 | async-start | bytes 262144 | tf_op jit(solution)/shard_map/all_to_all | solution.py:232
  58.3 3.2 %copy-start = (bf16[2048,2048]{1,0:T(8,128)(2,1)}, bf16[2048,2048]{1,0:T(8,128)(2,1)S(1)}, u32[]{:S(2)}) copy-start(bf16[2048,2048]{1,0:T(8,128)(2,1)S(1)} %get-tuple-element.23.high) | copy-start | bytes 25165828
  61.6 3.2 %copy-start.2 = (bf16[2048,2048]{1,0:T(8,128)(2,1)}, bf16[2048,2048]{1,0:T(8,128)(2,1)S(1)}, u32[]{:S(2)}) copy-start(bf16[2048,2048]{1,0:T(8,128)(2,1)S(1)} %get-tuple-element.24.low) | copy-start | bytes 25165828
  64.8 3.4 %copy-start.1 = (bf16[2048,2048]{1,0:T(8,128)(2,1)S(1)}, bf16[2048,2048]{1,0:T(8,128)(2,1)}, u32[]{:S(2)}) copy-start(bf16[2048,2048]{1,0:T(8,128)(2,1)} %copy-done) | copy-start | bytes 25165828
  68.2 3.4 %copy-start.3 = (bf16[2048,2048]{1,0:T(8,128)(2,1)S(1)}, bf16[2048,2048]{1,0:T(8,128)(2,1)}, u32[]{:S(2)}) copy-start(bf16[2048,2048]{1,0:T(8,128)(2,1)} %copy-done.2) | copy-start | bytes 25165828
  71.6 43.2 %copy-start.5 = (f32[128,128]{1,0:T(8,128)S(1)}, f32[128,128]{1,0:T(8,128)}, u32[]{:S(2)}) copy-start(f32[128,128]{1,0:T(8,128)} %leaf.5) | copy-start | bytes 196612

commit v2 on v1

--- a/solution.py
+++ b/solution.py
@@ -14,6 +14,7 @@
 G2 = ("zl", "y", "c")
 NG = 16
 NT = 8
+FIRST = 10
 COLS = 16
 PTS = 128
 RANK = 64
@@ -74,26 +75,53 @@
     return terms[0]
 
 
-def call(kernel, outs, *args, smem=0, limit=8 << 20, scratch=(), name=None):
-    specs = [pl.BlockSpec(memory_space=pltpu.SMEM)] * smem
-    specs += [pl.BlockSpec(memory_space=pltpu.VMEM)] * (len(args) - smem)
+VMEM = pltpu.MemorySpace.VMEM
+SMEM = pltpu.MemorySpace.SMEM
+HBM = pltpu.MemorySpace.HBM
+
+
+def call(kernel, outs, *args, spaces=None, out_spaces=None, limit=8 << 20, scratch=(), name=None):
+    spaces = spaces or [VMEM] * len(args)
+    out_spaces = out_spaces or [VMEM] * len(outs)
+    args = [pltpu.with_memory_space_constraint(a, m) if m is HBM else a for a, m in zip(args, spaces)]
     return pl.pallas_call(
         kernel,
-        out_shape=[jax.ShapeDtypeStruct(s, d) for s, d in outs],
-        in_specs=specs,
-        out_specs=[pl.BlockSpec(memory_space=pltpu.VMEM)] * len(outs),
+        out_shape=[m(s, d) if m is HBM else jax.ShapeDtypeStruct(s, d) for m, (s, d) in zip(out_spaces, outs)],
+        in_specs=[pl.BlockSpec(memory_space=m) for m in spaces],
+        out_specs=[pl.BlockSpec(memory_space=m) for m in out_spaces],
         scratch_shapes=list(scratch),
         compiler_params=pltpu.CompilerParams(vmem_limit_bytes=limit),
         name=name,
     )(*args)
 
 
-def start_kernel(points, inv, target, bits, top, sub, send, rhs, basis):
+def start_kernel(tid, inv_h, points_h, target_h, bits_h, top_h, sub_h, leaf_h, send, rhs, basis, leaf, weights, points, target, bits, inv, sems):
+    moves = [
+        pltpu.make_async_copy(src, dst, sems.at[k])
+        for k, (src, dst) in enumerate(
+            [
+                (bits_h, bits),
+                (target_h, target),
+                (top_h, basis.at[pl.ds(0, RANK)]),
+                (sub_h, basis.at[pl.ds(RANK, RANK)]),
+                (points_h, points),
+                (inv_h, inv),
+                (leaf_h, leaf),
+            ]
+        )
+    ]
+    for m in moves:
+        m.start()
+    mine = (lane((NT, PTS)) < RANK) | (sublane((NT, PTS)) == tid[0])
+    weights[...] = jnp.where(mine, 1.0, 0.0)
+    for m in moves:
+        m.wait()
+    scale = jnp.zeros((COLS, PTS), F32)
+    for k in range(COLS):
+        scale = jnp.where(sublane((COLS, PTS)) == k, inv[k], scale)
     rhs[0:1, :] = target[...]
     rhs[1:COLS, :] = 2.0 * bits[...].astype(F32) - 1.0
-    basis[0:RANK, :] = top[...]
-    basis[RANK : 2 * RANK, :] = sub[...]
-    send[0:COLS, :] = points[...] * inv[...]
+    send[0:COLS, :] = points[...] * scale
     send[COLS : 2 * COLS, :] = dot_nt(rhs[...], basis[...])
 
 
@@ -108,14 +136,13 @@
         table[t] = got[2 * t, first : first + COLS] + got[2 * t + 1, first : first + COLS]
 
 
-def own_coefs(table, mine):
-    top = lane((COLS, PTS)) < RANK
-    return tree_sum([jnp.where(top | (mine == t), table[t], 0.0) for t in range(NT)])
-
-
-def precond0_kernel(tid, got, rhs, leaf, basis, z, table):
+def own_coefs(table, weights):
+    return tree_sum([table[t] * weights[t : t + 1, :] for t in range(NT)])
+
+
+def precond0_kernel(got, rhs, leaf, basis, weights, z, table):
     subtree_table(got, COLS, table)
-    coefs = own_coefs(table, tid[0])
+    coefs = own_coefs(table, weights)
     z[...] = dot_nt(rhs[...], leaf[...]) + dot_nn(coefs, basis[...])
 
 
@@ -139,30 +166,54 @@
     return jnp.concatenate(parts + [tail, jnp.zeros((PTS - 6 * COLS - 8, PTS), F32)], 0)
 
 
-def matern_kernel(left, right, high, low, left_f, right_f):
+def matern_rows(lhs, right_f, high, low):
+    width = 256
+    for j in range(0, NG * PTS, width):
+        s = jnp.dot(lhs, right_f[:, j : j + width], preferred_element_type=F32)
+        s = jnp.maximum(s, 1e-30)
+        v = s * lax.rsqrt(s)
+        k = ((LN2 * LN2 / 3.0 * s + 1.0) + LN2 * v) * jnp.exp2(-v)
+        h = k.astype(BF16)
+        high[:, j : j + width] = h
+        low[:, j : j + width] = (k - h.astype(F32)).astype(BF16)
+
+
+def slab(i):
+    return pl.ds(pl.multiple_of(i * PTS, PTS), PTS)
+
+
+def matern_first_kernel(left, right, high_h, low_h, left_f, right_f, high, low, sems):
     for j in range(NG):
         at = slice(j * PTS, (j + 1) * PTS)
         right_f[:, at] = features(right[j, 0:COLS] * COORD_SCALE, False).astype(BF16)
         left_f[at, :] = features(left[j, 0:COLS] * COORD_SCALE, True).T.astype(BF16)
-    width = 256
+
+    def moves(i, slot):
+        return (
+            pltpu.make_async_copy(high.at[slot], high_h.at[slab(i)], sems.at[slot, 0]),
+            pltpu.make_async_copy(low.at[slot], low_h.at[slab(i)], sems.at[slot, 1]),
+        )
 
     def step(i, carry):
-        rows = pl.ds(pl.multiple_of(i * PTS, PTS), PTS)
-        lhs = left_f[rows, :]
-        for j in range(0, NG * PTS, width):
-            s = jnp.dot(lhs, right_f[:, j : j + width], preferred_element_type=F32)
-            s = jnp.maximum(s, 1e-30)
-            v = s * lax.rsqrt(s)
-            k = ((LN2 * LN2 / 3.0 * s + 1.0) + LN2 * v) * jnp.exp2(-v)
-            h = k.astype(BF16)
-            high[rows, j : j + width] = h
-            low[rows, j : j + width] = (k - h.astype(F32)).astype(BF16)
+        slot = i % 2
+
+        @pl.when(i >= 2)
+        def _():
+            for m in moves(i - 2, slot):
+                m.wait()
+
+        matern_rows(left_f[slab(i), :], right_f, high.at[slot], low.at[slot])
+        for m in moves(i, slot):
+            m.start()
         return carry
 
-    lax.fori_loop(0, NG, step, 0)
-
-
-def matvec_kernel(got, high, low, out):
+    lax.fori_loop(0, FIRST, step, 0)
+    for i in (FIRST - 2, FIRST - 1):
+        for m in moves(i, i % 2):
+            m.wait()
+
+
+def matvec_rows(got, high, low, out):
     v = jnp.concatenate([got[j] for j in range(NG)], 1)
     v_high = v.astype(BF16)
     both = jnp.concatenate([v_high, (v - v_high.astype(F32)).astype(BF16)], 0)
@@ -174,19 +225,38 @@
             out[j // PTS + b] = r[:, b * PTS : (b + 1) * PTS]
 
 
+def matern_rest_kernel(got, left_f, right_f, high_h, low_h, out, high, low, sems):
+    done = pl.ds(0, FIRST * PTS)
+    moves = (
+        pltpu.make_async_copy(high_h, high.at[done], sems.at[0]),
+        pltpu.make_async_copy(low_h, low.at[done], sems.at[1]),
+    )
+    for m in moves:
+        m.start()
+
+    def step(i, carry):
+        matern_rows(left_f[slab(i), :], right_f, high.at[slab(i)], low.at[slab(i)])
+        return carry
+
+    lax.fori_loop(FIRST, NG, step, 0)
+    for m in moves:
+        m.wait()
+    matvec_rows(got, high, low, out)
+
+
 def image0_kernel(got, z, rhs, basis, q, send):
     q[...] = tree_sum([got[j] for j in range(NG)]) + NOISE * z[...]
     send[0:COLS, :] = dot_nt(q[...], basis[...])
     send[COLS:, :] = tile_rows([pack([rowdot(rhs[...], z[...]), rowdot(z[...], q[...])])])
 
 
-def precond1_kernel(tid, got, rhs, q, leaf, basis, table0, z, res, table, table_q, sums):
+def precond1_kernel(got, rhs, q, leaf, basis, weights, table0, z, res, table, table_q, sums):
     sums[...] = tree_sum([got[j, COLS:] for j in range(NG)])
     alpha = unpack(sums[0:1, :], 0) / unpack(sums[0:1, :], 1)
     subtree_table(got, 0, table_q)
     for t in range(NT):
         table[t] = table0[t] - alpha * table_q[t]
-    coefs = own_coefs(table, tid[0])
+    coefs = own_coefs(table, weights)
     res[...] = rhs[...] - alpha * q[...]
     z[...] = dot_nt(res[...], leaf[...]) + dot_nn(coefs, basis[...])
 
@@ -232,43 +302,55 @@
     return lax.all_to_all(jnp.broadcast_to(block[None], (NG,) + block.shape), axes, 0, 0, tiled=True)
 
 
-def on_device(points, inverse_length, target, probe_bits, leaf, top_basis, sub_basis):
+def scatter(parts):
+    return lax.all_to_all(parts, G2, 0, 0, tiled=True)
+
+
+def on_device(points, inverse_length, target, probe_bits, leaf_inverse, top_basis, sub_basis):
     vec = ((COLS, PTS), F32)
+    square = ((PTS, PTS), F32)
     table = ((NT, COLS, PTS), F32)
+    part = ((FIRST * PTS, NG * PTS), BF16)
     block = ((NG * PTS, NG * PTS), BF16)
+    parts = ((NG, COLS, PTS), F32)
+    double = ((2 * COLS, PTS), F32)
+    wide = ((COLS + 8, PTS), F32)
+    dma = pltpu.SemaphoreType.DMA
     tid = lax.axis_index(("zl", "y")).astype(jnp.int32).reshape(1)
-    send, rhs, basis = call(
+    send, rhs, basis, leaf, weights = call(
         start_kernel,
-        [((2 * COLS, PTS), F32), vec, ((2 * RANK, PTS), F32)],
-        points, inverse_length[:, None], target[None, :], probe_bits, top_basis, sub_basis,
+        [double, vec, square, square, ((NT, PTS), F32)],
+        tid, inverse_length, points, target[None, :], probe_bits, top_basis, sub_basis, leaf_inverse,
+        spaces=[SMEM] + [HBM] * 7,
+        scratch=[
+            pltpu.VMEM((COLS, PTS), F32), pltpu.VMEM((1, PTS), F32), pltpu.VMEM((COLS - 1, PTS), jnp.int32),
+            pltpu.SMEM((COLS,), F32), dma((7,)),
+        ],
         name="start",
     )
     got1 = gather(send, G1)
-    (send,) = call(functools.partial(fold_kernel, COLS), [((2 * COLS, PTS), F32)], got1, send, name="fold0")
+    (send,) = call(functools.partial(fold_kernel, COLS), [double], got1, send, name="fold0")
     got2 = gather(send, G2)
-    z0, table0 = call(precond0_kernel, [vec, table], tid, got2, rhs, leaf, basis, smem=1, name="precond0")
+    z0, table0 = call(precond0_kernel, [vec, table], got2, rhs, leaf, basis, weights, name="precond0")
     dirs = gather(z0, G1)
-    high, low = call(
-        matern_kernel, [block, block], got1, got2,
-        limit=24 << 20,
-        scratch=[pltpu.VMEM((NG * PTS, PTS), BF16), pltpu.VMEM((PTS, NG * PTS), BF16)],
-        name="matern",
-    )
-
-    def matvec(dirs):
-        (parts,) = call(matvec_kernel, [((NG, COLS, PTS), F32)], dirs, high, low, limit=24 << 20, name="matvec")
-        return lax.all_to_all(parts, G2, 0, 0, tiled=True)
-
-    wide = ((COLS + 8, PTS), F32)
-    q, send = call(image0_kernel, [vec, wide], matvec(dirs), z0, rhs, basis, name="image0")
+    high_h, low_h, left_f, right_f = call(
+        matern_first_kernel, [part, part, ((NG * PTS, PTS), BF16), ((PTS, NG * PTS), BF16)], got1, got2,
+        out_spaces=[HBM, HBM, VMEM, VMEM],
+        scratch=[pltpu.VMEM((2, PTS, NG * PTS), BF16), pltpu.VMEM((2, PTS, NG * PTS), BF16), dma((2, 2))],
+        name="matern_first",
+    )
+    out, high, low = call(
+        matern_rest_kernel, [parts, block, block], dirs, left_f, right_f, high_h, low_h,
+        spaces=[VMEM] * 3 + [HBM] * 2, limit=24 << 20, scratch=[dma((2,))], name="matern_rest",
+    )
+    q, send = call(image0_kernel, [vec, wide], scatter(out), z0, rhs, basis, name="image0")
     (send,) = call(functools.partial(fold_kernel, 0), [wide], gather(send, G1), send, name="fold1")
     z1, res, table1, table_q, sums0 = call(
         precond1_kernel, [vec, vec, table, table, ((8, PTS), F32)],
-        tid, gather(send, G2), rhs, q, leaf, basis, table0, smem=1, name="precond1",
-    )
-    p, send = call(
-        image1_kernel, [vec, wide], matvec(gather(z1, G1)), z1, z0, res, q, leaf, basis, name="image1"
-    )
+        gather(send, G2), rhs, q, leaf, basis, weights, table0, name="precond1",
+    )
+    (out,) = call(matvec_rows, [parts], gather(z1, G1), high, low, limit=24 << 20, name="matvec")
+    p, send = call(image1_kernel, [vec, wide], scatter(out), z1, z0, res, q, leaf, basis, name="image1")
     (send,) = call(functools.partial(fold_kernel, 0), [wide], gather(send, G1), send, name="fold2")
     x_out, r_out, coefs = call(
         finish_kernel, [vec, vec, ((2, 2, COLS), F32)],

time: 168 us -> 153 us (0.911)
  local copies, waits for them, and re-layouts: 19.9 us -> 0.83 us
  blocking collectives: 110 us -> 125 us
  starting transfers between devices: 11.8 us -> 3.7 us
  waiting for transfers between devices: 7.2 us -> 0.15 us
  Pallas kernels: 17.6 us -> 21.6 us
    unnamed x22 -> x0, local copies, waits for them, and re-layouts: 17.6 us -> none
    all_to_all x6 -> x7, blocking collectives: 89.3 us -> 103 us  [gather(): lax.all_to_all(jnp.broadcast_to(block[None], (NG,) + block.shape), axes,...]
    all_to_all x2 -> x1, starting transfers between devices: 11.8 us -> 3.7 us  [gather(): lax.all_to_all(jnp.broadcast_to(block[None], (NG,) + block.shape), axes,...]
    all_to_all x2 -> x1, waiting for transfers between devices: 7.2 us -> 0.15 us  [gather(): lax.all_to_all(jnp.broadcast_to(block[None], (NG,) + block.shape), axes,...]
    pallas_call x12, Pallas kernels: 17.6 us -> 21.6 us  [call(): pl.pallas_call(kernel, out_shape=[m(s, d) if m is HBM else jax.ShapeDtype...]
  transfers between devices with their start and end apart: 2 -> 1, of which waited for: 1 -> 1; matrix products, arithmetic and copies ran while one was open for 0% -> 0% of each run, Pallas kernels for 6% -> 6%
where the time goes in v2:
time: 153 us; the launch traced here: 152 us
  blocking collectives  125 us (82%)
  Pallas kernels  21.6 us (14%)
  starting transfers between devices  3.7 us (2%)
    all_to_all x7, blocking collectives, gather(): lax.all_to_all(jnp.broadcast_to(block[None], (NG,) + block.shape), axes,...  103 us
    all_to_all x2, blocking collectives, scatter(): return lax.all_to_all(parts, G2, 0, 0, tiled=True)  22.1 us
    pallas_call x12, Pallas kernels, call(): pl.pallas_call(kernel, out_shape=[m(s, d) if m is HBM else jax.ShapeDtype...  21.6 us
    all_to_all x1, starting transfers between devices, gather(): lax.all_to_all(jnp.broadcast_to(block[None], (NG,) + block.shape), axes,...  3.7 us
  transfers between devices with their start and end apart: 1, of which 1 were waited for; matrix products, arithmetic and copies ran while one was open for 0% of the time, Pallas kernels for 6%

profile of v2, /device:TPU:1, one launch (start us, length us, event | category | flops | bytes accessed | tf_op | source)
XLA Modules:
  0.0 152.0 jit_solution(279364228470420576)
XLA Ops:
  0.6 1.2 start.1
  1.9 21.5 %all_to_all.50.got.left = f32[16,32,128]{2,1,0:T(8,128)S(1)} all-to-all(f32[16,32,128]{2,1,0:T(8,128)S(1)} %broadcast_in_dim.19), channel_id=1, replica_groups=mesh['zl'=2,'y'=4,'zh'=4,'x'=4,'c'=2] {'zh','x'}, dimensions={0} | all-to-all | bytes 524288 | tf_op jit(solution)/shard_map/all_to_all | solution.py:302
  23.4 15.0 %all_to_all.51.got.right = f32[16,32,128]{2,1,0:T(8,128)S(1)} all-to-all(f32[16,32,128]{2,1,0:T(8,128)S(1)} %broadcast_in_dim.20), channel_id=1, replica_groups=mesh['zl'=2,'y'=4,'zh'=4,'x'=4,'c'=2] {'zl','y','c'}, dimensions={0} | all-to-all | bytes 524288 | tf_op jit(solution)/shard_map/all_to_all | solution.py:302
  38.5 0.3 precond0.1
  38.7 0.7 broadcast_in_dim.21
  39.4 3.7 %all-to-all-start.2 = ((f32[16,16,128]{2,1,0:T(8,128)}), f32[16,16,128]{2,1,0:T(8,128)S(1)}, u32[]{:S(2)}, u32[]{:S(2)}) async-start(f32[16,16,128]{2,1,0:T(8,128)} %broadcast_in_dim.21), calls=%async_computation.2 | async-start | bytes 262144 | tf_op jit(solution)/shard_map/all_to_all | solution.py:302
  43.1 9.1 %matern_first.1 = (bf16[1280,2048]{1,0:T(8,128)(2,1)}, bf16[1280,2048]{1,0:T(8,128)(2,1)}, bf16[2048,128]{1,0:T(8,128)(2,1)S(1)}, bf16[128,2048]{1,0:T(8,128)(2,1)S(1)}) custom-call(f32[16,32,128]{2,1,0:T(8,128)S(1)} %all_to_all.50.got.left, f32[16,32,128]{2,1,0:T(8,128)S(1)} %all_to_all.51.got.right), custom_call_target="tpu_custom_call" | custom-call | tf_op jit(solution)/shard_map/matern_first/pallas_call | solution.py:87
  52.2 0.1 all-to-all-done.2.got
  52.4 6.6 %matern_rest.1 = (f32[16,16,128]{2,1,0:T(8,128)S(1)}, bf16[2048,2048]{1,0:T(8,128)(2,1)S(1)}, bf16[2048,2048]{1,0:T(8,128)(2,1)S(1)}) custom-call(f32[16,16,128]{2,1,0:T(8,128)S(1)} %all-to-all-done.2.got, bf16[2048,128]{1,0:T(8,128)(2,1)S(1)} %get-tuple-element.32.left_f, bf16[128,2048]{1,0:T(8,128)(2,1)S(1)} %get-tuple-element.33.right_f, ...), custom_call_target="tpu_custom_call" | custom-call | tf_op jit(solution)/shard_map/matern_rest/pallas_call | solution.py:87
  59.0 11.2 %all_to_all.52.got = f32[16,16,128]{2,1,0:T(8,128)S(1)} all-to-all(f32[16,16,128]{2,1,0:T(8,128)S(1)} %get-tuple-element.36), channel_id=1, replica_groups=mesh['zl'=2,'y'=4,'zh'=4,'x'=4,'c'=2] {'zl','y','c'}, dimensions={0} | all-to-all | bytes 262144 | tf_op jit(solution)/shard_map/all_to_all | solution.py:306
  70.1 0.2 image0.1
  70.4 17.3 %all_to_all.53.got = f32[16,24,128]{2,1,0:T(8,128)S(1)} all-to-all(f32[16,24,128]{2,1,0:T(8,128)S(1)} %broadcast_in_dim.22), channel_id=1, replica_groups=mesh['zl'=2,'y'=4,'zh'=4,'x'=4,'c'=2] {'zh','x'}, dimensions={0} | all-to-all | bytes 393216 | tf_op jit(solution)/shard_map/all_to_all | solution.py:302
  87.7 11.9 %all_to_all.54.got = f32[16,24,128]{2,1,0:T(8,128)S(1)} all-to-all(f32[16,24,128]{2,1,0:T(8,128)S(1)} %broadcast_in_dim.23), channel_id=1, replica_groups=mesh['zl'=2,'y'=4,'zh'=4,'x'=4,'c'=2] {'zl','y','c'}, dimensions={0} | all-to-all | bytes 393216 | tf_op jit(solution)/shard_map/all_to_all | solution.py:302
  99.6 0.3 precond1.1
  100.0 12.7 %all_to_all.55.got = f32[16,16,128]{2,1,0:T(8,128)S(1)} all-to-all(f32[16,16,128]{2,1,0:T(8,128)S(1)} %broadcast_in_dim.24), channel_id=1, replica_groups=mesh['zl'=2,'y'=4,'zh'=4,'x'=4,'c'=2] {'zh','x'}, dimensions={0} | all-to-all | bytes 262144 | tf_op jit(solution)/shard_map/all_to_all | solution.py:302
  112.6 2.5 %matvec.1 = f32[16,16,128]{2,1,0:T(8,128)S(1)} custom-call(f32[16,16,128]{2,1,0:T(8,128)S(1)} %all_to_all.55.got, bf16[2048,2048]{1,0:T(8,128)(2,1)S(1)} %get-tuple-element.41.high, bf16[2048,2048]{1,0:T(8,128)(2,1)S(1)} %get-tuple-element.42.low), custom_call_target="tpu_custom_call" | custom-call | tf_op jit(solution)/shard_map/matvec/pallas_call | solution.py:87
  115.1 10.9 %all_to_all.56.got = f32[16,16,128]{2,1,0:T(8,128)S(1)} all-to-all(f32[16,16,128]{2,1,0:T(8,128)S(1)} %matvec.1), channel_id=1, replica_groups=mesh['zl'=2,'y'=4,'zh'=4,'x'=4,'c'=2] {'zl','y','c'}, dimensions={0} | all-to-all | bytes 262144 | tf_op jit(solution)/shard_map/all_to_all | solution.py:306
  126.1 0.6 image1.1
  126.7 12.6 %all_to_all.57.got = f32[16,24,128]{2,1,0:T(8,128)S(1)} all-to-all(f32[16,24,128]{2,1,0:T(8,128)S(1)} %broadcast_in_dim.25), channel_id=1, replica_groups=mesh['zl'=2,'y'=4,'zh'=4,'x'=4,'c'=2] {'zh','x'}, dimensions={0} | all-to-all | bytes 393216 | tf_op jit(solution)/shard_map/all_to_all | solution.py:302
  139.4 11.9 %all_to_all.58.got = f32[16,24,128]{2,1,0:T(8,128)S(1)} all-to-all(f32[16,24,128]{2,1,0:T(8,128)S(1)} %broadcast_in_dim.26), channel_id=1, replica_groups=mesh['zl'=2,'y'=4,'zh'=4,'x'=4,'c'=2] {'zl','y','c'}, dimensions={0} | all-to-all | bytes 393216 | tf_op jit(solution)/shard_map/all_to_all | solution.py:302
  151.2 0.8 finish.1
  (10 shorter events, 0.2 us)
Async XLA Ops:
  39.4 12.9 %all-to-all-start.2 = ((f32[16,16,128]{2,1,0:T(8,128)}), f32[16,16,128]{2,1,0:T(8,128)S(1)}, u32[]{:S(2)}, u32[]{:S(2)}) async-start(f32[16,16,128]{2,1,0:T(8,128)} %broadcast_in_dim.21), calls=%async_computation.2 | async-start | bytes 262144 | tf_op jit(solution)/shard_map/all_to_all | solution.py:302

commit v3 on v2

v3 whole, which is shorter than its diff:
```python
import functools
import math

import jax
import jax.numpy as jnp
from jax import lax
from jax.experimental import pallas as pl
from jax.experimental.pallas import tpu as pltpu
from jax.sharding import Mesh
from jax.sharding import PartitionSpec as P

AXES = ("zl", "y", "zh", "x", "c")
GA = ("y", "x")
GB = ("zl", "zh", "c")
NG = 16
NT = 8
COLS = 16
PTS = 128
RANK = 64
NOISE = 0.5
F32 = jnp.float32
BF16 = jnp.bfloat16
LN2 = math.log(2.0)
COORD_SCALE = math.sqrt(5.0) / LN2
HIGHEST = lax.Precision.HIGHEST


def dot_nt(a, b):
    return lax.dot_general(a, b, (((1,), (1,)), ((), ())), precision=HIGHEST, preferred_element_type=F32)


def dot_nn(a, b):
    return lax.dot_general(a, b, (((1,), (0,)), ((), ())), precision=HIGHEST, preferred_element_type=F32)


def lane(shape):
    return lax.broadcasted_iota(jnp.int32, shape, 1)


def sublane(shape):
    return lax.broadcasted_iota(jnp.int32, shape, 0)


def pack(sums):
    shape = (COLS, PTS)
    acc = jnp.zeros(shape, F32)
    for k, s in enumerate(sums):
        acc = jnp.where(lane(shape) == COLS * k + sublane(shape), jnp.broadcast_to(s, shape), acc)
    return jnp.sum(acc, 0, keepdims=True)


def unpack(row, k):
    shape = (COLS, PTS)
    hit = lane(shape) == COLS * k + sublane(shape)
    return jnp.sum(jnp.where(hit, jnp.broadcast_to(row, shape), 0.0), 1, keepdims=True)


def rowdot(a, b):
    return jnp.sum(a * b, 1, keepdims=True)


def tile_rows(rows):
    shape = (8, PTS)
    out = jnp.zeros(shape, F32)
    for k, r in enumerate(rows):
        out = jnp.where(sublane(shape) == k, jnp.broadcast_to(r, shape), out)
    return out


def tree_sum(terms):
    terms = list(terms)
    while len(terms) > 1:
        terms = [terms[i] + terms[i + 1] if i + 1 < len(terms) else terms[i] for i in range(0, len(terms), 2)]
    return terms[0]


VMEM = pltpu.MemorySpace.VMEM
SMEM = pltpu.MemorySpace.SMEM
HBM = pltpu.MemorySpace.HBM


def call(kernel, outs, *args, spaces=None, out_spaces=None, limit=8 << 20, scratch=(), name=None):
    spaces = spaces or [VMEM] * len(args)
    out_spaces = out_spaces or [VMEM] * len(outs)
    args = [pltpu.with_memory_space_constraint(a, m) if m is HBM else a for a, m in zip(args, spaces)]
    return pl.pallas_call(
        kernel,
        out_shape=[m(s, d) if m is HBM else jax.ShapeDtypeStruct(s, d) for m, (s, d) in zip(out_spaces, outs)],
        in_specs=[pl.BlockSpec(memory_space=m) for m in spaces],
        out_specs=[pl.BlockSpec(memory_space=m) for m in out_spaces],
        scratch_shapes=list(scratch),
        compiler_params=pltpu.CompilerParams(vmem_limit_bytes=limit),
        name=name,
    )(*args)


SEND0 = 12 * COLS
BASES = slice(3 * COLS, 3 * COLS + PTS)
LEAF_PART = slice(11 * COLS, 12 * COLS)


def start_kernel(where, inv_h, points_h, target_h, bits_h, top_h, sub_h, leaf_h, send, rhs, basis, leaf, leaf_part, marks, points, target, bits, inv, sems):
    moves = [
        pltpu.make_async_copy(src, dst, sems.at[k])
        for k, (src, dst) in enumerate(
            [
                (bits_h, bits),
                (target_h, target),
                (top_h, basis.at[pl.ds(0, RANK)]),
                (sub_h, basis.at[pl.ds(RANK, RANK)]),
                (points_h, points),
                (inv_h, inv),
                (leaf_h, leaf),
            ]
        )
    ]
    for m in moves:
        m.start()
    row = sublane((NG + 8, PTS))
    place = where[0]
    hit = (row == lax.rem(place, NG)) | ((row >= NG) & (place >= NG))
    marks[...] = jnp.where(hit, 1.0, 0.0)
    for m in moves:
        m.wait()
    scale = jnp.zeros((COLS, PTS), F32)
    for k in range(COLS):
        scale = jnp.where(sublane((COLS, PTS)) == k, inv[k], scale)
    rhs[0:1, :] = target[...]
    rhs[1:COLS, :] = 2.0 * bits[...].astype(F32) - 1.0
    send[0:COLS, :] = points[...] * scale
    send[COLS : 2 * COLS, :] = dot_nt(rhs[...], basis[...])
    leaf_part[...] = dot_nt(rhs[...], leaf[...])


def fold_tiles(got, first, scalars, send, at):
    low = lane((COLS, PTS)) < RANK
    zero = tree_sum([got[j, first : first + COLS] for j in range(NG // 2)])
    one = tree_sum([got[j, first : first + COLS] for j in range(NG // 2, NG)])
    send[at : at + COLS, :] = jnp.where(low, zero + one, zero)
    send[at + COLS : at + 2 * COLS, :] = jnp.where(low, 0.0, one)
    if scalars:
        own = tree_sum([got[j, scalars : scalars + 8] for j in range(NG)])
        send[at + COLS : at + COLS + 8, :] = jnp.where(low[0:8], own, one[0:8])


def fold0_kernel(got, own, basis, leaf_part, send):
    send[0:COLS, :] = own[0:COLS, :]
    fold_tiles(got, COLS, 0, send, COLS)
    send[BASES, :] = basis[...]
    send[LEAF_PART, :] = leaf_part[...]


def fold1_kernel(got, leaf_part, send):
    fold_tiles(got, 0, COLS, send, 0)
    send[2 * COLS : 3 * COLS, :] = leaf_part[...]


def fold2_kernel(got, send):
    fold_tiles(got, 0, COLS, send, 0)


def sum_tiles(got, first):
    return [
        tree_sum([got[4 * y + x, at : at + COLS] for x in range(4)]) for at in (first, first + COLS) for y in range(4)
    ]


def column_directions(marks, table, leaf_parts, got0, directions):
    low = lane((COLS, PTS)) < RANK
    odd = marks[NG : NG + 1, :] > 0.5
    top = tree_sum(table[0:4])
    for y in range(4):
        coefs = jnp.where(low, top, jnp.where(odd, table[4 + y], table[y]))
        high = coefs.astype(BF16)
        both = jnp.concatenate([high, (coefs - high.astype(F32)).astype(BF16)], 0)
        for j in range(4 * y, 4 * y + 4):
            bases = got0[j, BASES]
            first = bases.astype(BF16)
            r = jnp.dot(both, first, preferred_element_type=F32)
            r = r[0:COLS] + r[COLS:] + jnp.dot(high, (bases - first.astype(F32)).astype(BF16), preferred_element_type=F32)
            directions[j] = leaf_parts(j) + r


def own_direction(marks, directions):
    return tree_sum([directions[j] * marks[j : j + 1, :] for j in range(NG)])


def features(x, left):
    def pieces(v):
        first = v.astype(BF16).astype(F32)
        second = (v - first).astype(BF16).astype(F32)
        third = (v - first - second).astype(BF16).astype(F32)
        return first, second, third

    a, b, c = pieces(x)
    norms = pieces(jnp.sum(x * x, 0, keepdims=True))
    ones = (jnp.ones((1, PTS), F32),) * 3
    if left:
        parts = [a, a, b, b, a, c]
        tail = tile_rows(norms + ones)
    else:
        a, b, c = -2.0 * a, -2.0 * b, -2.0 * c
        parts = [a, b, a, b, c, a]
        tail = tile_rows(ones + norms)
    return jnp.concatenate(parts + [tail, jnp.zeros((PTS - 6 * COLS - 8, PTS), F32)], 0)


def slab(i):
    return pl.ds(pl.multiple_of(i * PTS, PTS), PTS)


def matern_block(left, right, high, low, left_f, right_f):
    for j in range(NG):
        at = slice(j * PTS, (j + 1) * PTS)
        right_f[:, at] = features(right[j, 0:COLS] * COORD_SCALE, False).astype(BF16)
        left_f[at, :] = features(left[j, 0:COLS] * COORD_SCALE, True).T.astype(BF16)
    width = 256

    def step(i, carry):
        lhs = left_f[slab(i), :]
        for j in range(0, NG * PTS, width):
            s = jnp.dot(lhs, right_f[:, j : j + width], preferred_element_type=F32)
            s = jnp.maximum(s, 1e-30)
            v = s * lax.rsqrt(s)
            k = ((LN2 * LN2 / 3.0 * s + 1.0) + LN2 * v) * jnp.exp2(-v)
            h = k.astype(BF16)
            high[slab(i), j : j + width] = h
            low[slab(i), j : j + width] = (k - h.astype(F32)).astype(BF16)
        return carry

    lax.fori_loop(0, NG, step, 0)


def matvec(directions, high, low, out):
    v = jnp.concatenate([directions[j] for j in range(NG)], 1)
    v_high = v.astype(BF16)
    both = jnp.concatenate([v_high, (v - v_high.astype(F32)).astype(BF16)], 0)
    width = 512
    for j in range(0, NG * PTS, width):
        r = jnp.dot(both, high[:, j : j + width], preferred_element_type=F32)
        r = r[0:COLS] + r[COLS:] + jnp.dot(v_high, low[:, j : j + width], preferred_element_type=F32)
        for b in range(width // PTS):
            out[j // PTS + b] = r[:, b * PTS : (b + 1) * PTS]


def first_kernel(marks, got_a, got_b, out, high, low, z, table, directions, left_f, right_f):
    now = sum_tiles(got_a, COLS)
    for t in range(NT):
        table[t] = now[t]
    column_directions(marks, now, lambda j: got_a[j, LEAF_PART], got_a, directions)
    z[...] = own_direction(marks, directions)
    matern_block(got_a, got_b, high, low, left_f, right_f)
    matvec(directions, high, low, out)


def image0_kernel(got, z, rhs, basis, leaf, q, leaf_part, send):
    q[...] = tree_sum([got[j] for j in range(NG)]) + NOISE * z[...]
    send[0:COLS, :] = dot_nt(q[...], basis[...])
    send[COLS:, :] = tile_rows([pack([rowdot(rhs[...], z[...]), rowdot(z[...], q[...])])])
    leaf_part[...] = dot_nt(q[...], leaf[...])


def second_kernel(marks, got, got0, table0, rhs, q, high, low, out, z, res, table, table_q, sums, directions):
    now = sum_tiles(got, 0)
    total = tree_sum(now[4:8])
    sums[...] = total[0:8]
    alpha = unpack(total[0:1], 0) / unpack(total[0:1], 1)
    for t in range(NT):
        table_q[t] = now[t]
        now[t] = table0[t] - alpha * now[t]
        table[t] = now[t]
    column_directions(
        marks, now, lambda j: got0[j, LEAF_PART] - alpha * got[j, 2 * COLS : 3 * COLS], got0, directions
    )
    z[...] = own_direction(marks, directions)
    res[...] = rhs[...] - alpha * q[...]
    matvec(directions, high, low, out)


def image1_kernel(got, z1, z0, res, q, leaf, basis, p, send):
    p[...] = tree_sum([got[j] for j in range(NG)]) + NOISE * z1[...]
    send[0:COLS, :] = dot_nt(p[...], basis[...])
    rv, qv, pv, zv = res[...], q[...], p[...], z1[...]
    rb, qb, pb = (dot_nt(v, leaf[...]) for v in (rv, qv, pv))
    rows = [
        pack([rowdot(rv, zv), rowdot(zv, pv), rowdot(zv, qv), rowdot(z0[...], pv)]),
        pack([rowdot(rv, rb), rowdot(rv, qb), rowdot(rv, pb)]),
        pack([rowdot(qv, qb), rowdot(qv, pb), rowdot(pv, pb)]),
    ]
    send[COLS:, :] = tile_rows(rows)


def finish_kernel(got, z0, z1, res, q, p, table1, table_q, sums0, x_out, r_out, coefs):
    now = sum_tiles(got, 0)
    sums = tree_sum(now[4:8])
    rz0, z0q = unpack(sums0[0:1, :], 0), unpack(sums0[0:1, :], 1)
    rz1, z1p, z1q, z0p = (unpack(sums[0:1], k) for k in range(4))
    rbr, rbq, rbp = (unpack(sums[1:2], k) for k in range(3))
    qbq, qbp, pbp = (unpack(sums[2:3], k) for k in range(3))
    alpha0 = rz0 / z0q
    beta0 = rz1 / rz0
    alpha1 = rz1 / (z1p + beta0 * (z1q + z0p) + beta0 * beta0 * z0q)
    image = p[...] + beta0 * q[...]
    r_out[...] = res[...] - alpha1 * image
    x_out[...] = alpha0 * z0[...] + alpha1 * (z1[...] + beta0 * z0[...])
    leaf_part = (
        rbr
        - 2.0 * alpha1 * (rbp + beta0 * rbq)
        + alpha1 * alpha1 * (pbp + 2.0 * beta0 * qbp + beta0 * beta0 * qbq)
    )
    low = lane((COLS, PTS)) < RANK
    now = [table1[t] - alpha1 * (now[t] + beta0 * table_q[t]) for t in range(NT)]
    top = jnp.where(low, tree_sum(now[0:4]), 0.0)
    squares = top * top + tree_sum([jnp.where(low, 0.0, v * v) for v in now])
    beta1 = (leaf_part + jnp.sum(squares, 1, keepdims=True)) / rz1
    for k, v in enumerate((alpha0, alpha1, beta0, beta1)):
        coefs[k // 2, k % 2 : k % 2 + 1, :] = pack([v])[:, 0:COLS]


def gather(block, axes):
    return lax.all_to_all(jnp.broadcast_to(block[None], (NG,) + block.shape), axes, 0, 0, tiled=True)


def scatter(parts):
    return lax.all_to_all(parts, GB, 0, 0, tiled=True)


def on_device(points, inverse_length, target, probe_bits, leaf_inverse, top_basis, sub_basis):
    vec = ((COLS, PTS), F32)
    square = ((PTS, PTS), F32)
    table = ((NT, COLS, PTS), F32)
    block = ((NG * PTS, NG * PTS), BF16)
    parts = ((NG, COLS, PTS), F32)
    wide = ((COLS + 8, PTS), F32)
    dma = pltpu.SemaphoreType.DMA
    where = lax.axis_index(("zl",) + GA).astype(jnp.int32).reshape(1)
    send, rhs, basis, leaf, leaf_part, marks = call(
        start_kernel,
        [((2 * COLS, PTS), F32), vec, square, square, vec, ((NG + 8, PTS), F32)],
        where, inverse_length, points, target[None, :], probe_bits, top_basis, sub_basis, leaf_inverse,
        spaces=[SMEM] + [HBM] * 7,
        scratch=[
            pltpu.VMEM((COLS, PTS), F32), pltpu.VMEM((1, PTS), F32), pltpu.VMEM((COLS - 1, PTS), jnp.int32),
            pltpu.SMEM((COLS,), F32), dma((7,)),
        ],
        name="start",
    )
    got_b = gather(send, GB)
    (send,) = call(fold0_kernel, [((SEND0, PTS), F32)], got_b, send, basis, leaf_part, name="fold0")
    got_a = gather(send, GA)
    out, high, low, z0, table0 = call(
        first_kernel, [parts, block, block, vec, table], marks, got_a, got_b, limit=24 << 20,
        scratch=[
            pltpu.VMEM((NG, COLS, PTS), F32), pltpu.VMEM((NG * PTS, PTS), BF16), pltpu.VMEM((PTS, NG * PTS), BF16)
        ],
        name="first",
    )
    q, leaf_part, send = call(image0_kernel, [vec, vec, wide], scatter(out), z0, rhs, basis, leaf, name="image0")
    (send,) = call(fold1_kernel, [((3 * COLS, PTS), F32)], gather(send, GB), leaf_part, name="fold1")
    out, z1, res, table1, table_q, sums0 = call(
        second_kernel, [parts, vec, vec, table, table, ((8, PTS), F32)],
        marks, gather(send, GA), got_a, table0, rhs, q, high, low,
        limit=24 << 20, scratch=[pltpu.VMEM((NG, COLS, PTS), F32)], name="second",
    )
    p, send = call(image1_kernel, [vec, wide], scatter(out), z1, z0, res, q, leaf, basis, name="image1")
    (send,) = call(fold2_kernel, [((2 * COLS, PTS), F32)], gather(send, GB), name="fold2")
    x_out, r_out, coefs = call(
        finish_kernel, [vec, vec, ((2, 2, COLS), F32)],
        gather(send, GA), z0, z1, res, q, p, table1, table_q, sums0, name="finish",
    )
    return x_out, r_out, coefs


def solution(mesh):
    named = Mesh(mesh.devices.reshape(2, 4, 4, 4, 2), AXES)
    return jax.shard_map(
        on_device,
        mesh=named,
        in_specs=(P(None, AXES), P(), P(AXES), P(None, AXES), P(AXES, None), P(None, AXES), P(None, AXES)),
        out_specs=(P(None, AXES), P(None, AXES), P()),
        check_vma=False,
    )
```

time: 153 us -> 147 us (0.961)
  starting transfers between devices: 3.7 us -> 0 us
  Pallas kernels: 21.6 us -> 18.8 us
  blocking collectives: 125 us -> 127 us
    all_to_all x1 -> x0, starting transfers between devices: 3.7 us -> none  [gather(): lax.all_to_all(jnp.broadcast_to(block[None], (NG,) + block.shape), axes,...]
    pallas_call x12 -> x9, Pallas kernels: 21.6 us -> 18.8 us  [call(): pl.pallas_call(kernel, out_shape=[m(s, d) if m is HBM else jax.ShapeDtype...]
    all_to_all x2, blocking collectives: 22.1 us -> 24 us  [scatter(): return lax.all_to_all(parts, GB, 0, 0, tiled=True)]
    all_to_all x7 -> x6, blocking collectives: 103 us -> 103 us  [gather(): lax.all_to_all(jnp.broadcast_to(block[None], (NG,) + block.shape), axes,...]
  transfers between devices with their start and end apart: 1 -> 0, of which waited for: 1 -> 0; matrix products, arithmetic and copies ran while one was open for 0% -> 0% of each run, Pallas kernels for 6% -> 0%
where the time goes in v3:
time: 147 us; the launch traced here: 146 us
  blocking collectives  127 us (86%)
  Pallas kernels  18.8 us (13%)
    all_to_all x6, blocking collectives, gather(): lax.all_to_all(jnp.broadcast_to(block[None], (NG,) + block.shape), axes,...  103 us
    all_to_all x2, blocking collectives, scatter(): return lax.all_to_all(parts, GB, 0, 0, tiled=True)  24 us
    pallas_call x9, Pallas kernels, call(): pl.pallas_call(kernel, out_shape=[m(s, d) if m is HBM else jax.ShapeDtype...  18.8 us

profile of v3, /device:TPU:1, one launch (start us, length us, event | category | flops | bytes accessed | tf_op | source)
XLA Modules:
  0.0 146.3 jit_solution(10134819021510272614)
XLA Ops:
  0.6 1.3 start.1
  2.0 21.6 %all_to_all.40.got.got_b = f32[16,32,128]{2,1,0:T(8,128)S(1)} all-to-all(f32[16,32,128]{2,1,0:T(8,128)S(1)} %broadcast_in_dim.15), channel_id=1, replica_groups=mesh['zl'=2,'y'=4,'zh'=4,'x'=4,'c'=2] {'zl','zh','c'}, dimensions={0} | all-to-all | bytes 524288 | tf_op jit(solution)/shard_map/all_to_all | solution.py:321
  23.6 0.1 broadcast_in_dim.16
  23.8 30.3 %all_to_all.41.got_a.got0 = f32[16,192,128]{2,1,0:T(8,128)S(1)} all-to-all(f32[16,192,128]{2,1,0:T(8,128)S(1)} %broadcast_in_dim.16), channel_id=1, replica_groups=mesh['zl'=2,'y'=4,'zh'=4,'x'=4,'c'=2] {'y','x'}, dimensions={0} | all-to-all | bytes 3145728 | tf_op jit(solution)/shard_map/all_to_all | solution.py:321
  54.1 12.8 %first.1 = (f32[16,16,128]{2,1,0:T(8,128)S(1)}, bf16[2048,2048]{1,0:T(8,128)(2,1)S(1)}, bf16[2048,2048]{1,0:T(8,128)(2,1)S(1)}, f32[16,128]{1,0:T(8,128)S(1)}, f32[8,16,128]{2,1,0:T(8,128)S(1)}) custom-call(f32[24,128]{1,0:T(8,128)S(1)} %get-tuple-element.25.marks, f32[16,192,128]{2,1,0:T(8,128)S(1)} %all_to_all.41.got_a.got0, ...), custom_call_target="tpu_custom_call" | custom-call | tf_op jit(solution)/shard_map/first/pallas_call | solution.py:86
  67.0 11.9 %all_to_all.42.got = f32[16,16,128]{2,1,0:T(8,128)S(1)} all-to-all(f32[16,16,128]{2,1,0:T(8,128)S(1)} %get-tuple-element.29), channel_id=1, replica_groups=mesh['zl'=2,'y'=4,'zh'=4,'x'=4,'c'=2] {'zl','zh','c'}, dimensions={0} | all-to-all | bytes 262144 | tf_op jit(solution)/shard_map/all_to_all | solution.py:325
  78.9 0.3 image0.1
  79.2 13.0 %all_to_all.43.got = f32[16,24,128]{2,1,0:T(8,128)S(1)} all-to-all(f32[16,24,128]{2,1,0:T(8,128)S(1)} %broadcast_in_dim.17), channel_id=1, replica_groups=mesh['zl'=2,'y'=4,'zh'=4,'x'=4,'c'=2] {'zl','zh','c'}, dimensions={0} | all-to-all | bytes 393216 | tf_op jit(solution)/shard_map/all_to_all | solution.py:321
  92.2 13.1 %all_to_all.44.got = f32[16,48,128]{2,1,0:T(8,128)S(1)} all-to-all(f32[16,48,128]{2,1,0:T(8,128)S(1)} %broadcast_in_dim.18), channel_id=1, replica_groups=mesh['zl'=2,'y'=4,'zh'=4,'x'=4,'c'=2] {'y','x'}, dimensions={0} | all-to-all | bytes 786432 | tf_op jit(solution)/shard_map/all_to_all | solution.py:321
  105.4 2.9 %second.1 = (f32[16,16,128]{2,1,0:T(8,128)S(1)}, f32[16,128]{1,0:T(8,128)S(1)}, f32[16,128]{1,0:T(8,128)S(1)}, f32[8,16,128]{2,1,0:T(8,128)S(1)}, f32[8,16,128]{2,1,0:T(8,128)S(1)}, /*index=5*/f32[8,128]{1,0:T(8,128)S(1)}) custom-call(f32[24,128]{1,0:T(8,128)S(1)} %get-tuple-element.25.marks, f32[16,48,128]{2,1,0:T(8,128)S(1)} %all_to_all.44.got, ...), custom_call_target="tpu_custom_call" | custom-call | tf_op jit(solution)/shard_map/second/pallas_call | solution.py:86
  108.2 12.1 %all_to_all.45.got = f32[16,16,128]{2,1,0:T(8,128)S(1)} all-to-all(f32[16,16,128]{2,1,0:T(8,128)S(1)} %get-tuple-element.39), channel_id=1, replica_groups=mesh['zl'=2,'y'=4,'zh'=4,'x'=4,'c'=2] {'zl','zh','c'}, dimensions={0} | all-to-all | bytes 262144 | tf_op jit(solution)/shard_map/all_to_all | solution.py:325
  120.3 0.6 image1.1
  120.9 13.0 %all_to_all.46.got = f32[16,24,128]{2,1,0:T(8,128)S(1)} all-to-all(f32[16,24,128]{2,1,0:T(8,128)S(1)} %broadcast_in_dim.19), channel_id=1, replica_groups=mesh['zl'=2,'y'=4,'zh'=4,'x'=4,'c'=2] {'zl','zh','c'}, dimensions={0} | all-to-all | bytes 393216 | tf_op jit(solution)/shard_map/all_to_all | solution.py:321
  134.0 11.6 %all_to_all.47.got = f32[16,32,128]{2,1,0:T(8,128)S(1)} all-to-all(f32[16,32,128]{2,1,0:T(8,128)S(1)} %broadcast_in_dim.20), channel_id=1, replica_groups=mesh['zl'=2,'y'=4,'zh'=4,'x'=4,'c'=2] {'y','x'}, dimensions={0} | all-to-all | bytes 524288 | tf_op jit(solution)/shard_map/all_to_all | solution.py:321
  145.5 0.8 finish.1
  (8 shorter events, 0.2 us)
